TPU v7x, 32 devices: a whole 2x2x4 slice. The times are simulated.
32 devices in a mesh: region: 2 (over x), shard: 16 (over z, y, core).
Axes of the slice: x: 2, y: 2, z: 4, core: 2. Of those that a mesh axis runs over, the one named last changes fastest.
Arguments:
- queries: bfloat16 [48, 1024], replicated, may hold values from -6 to 6
- database: bfloat16 [16384, 1024], P(('region', 'shard')), may hold values from -6 to 6
- neighbour_ids: int32 [48, 10], replicated, may hold values from 0 to 16383
- tile_weights: bfloat16 [64, 13, 4, 256], P(('region', 'shard')), may hold values from 0.0019989014 to 0.059814453
- tile_columns: int32 [64, 13, 4, 256], P(('region', 'shard')), may hold values from 0 to 255
- tile_owner: int32 [64, 13], P(('region', 'shard')), may hold values from 0 to 15, all different within a row; in each aligned block of 2 rows (0 to 1, 2 to 3, ...) at most 2 rows name the same one
- tile_block: int32 [64, 13], P(('region', 'shard')), may hold values from 0 to 1
Outputs:
- diffused: float32 [48, 16384], P(None, ('region', 'shard'))
Inputs may be any that keep to these rules, and one draw needn't show every extreme that they name: `tile_owner`: each row names 13 different owners; among the rows of one device's blocks no owner is named more than 2 times, and that many in some devices.
All inputs are finite; a program needn't handle non-finite values.
Results may differ from a plain program's by a relative error of at most 0.005.
Values may be sent and summed in bfloat16 or wider, within the bound.
A program may use at most 64 MiB of HBM per device.

v0:
```python
import math
import jax
import jax.numpy as jnp
from jax import lax
from jax.sharding import PartitionSpec as P

EPS = 1e-06
BETA = 0.8


def unit_rows(matrix):
    return matrix / jnp.sqrt(jnp.sum(matrix * matrix, axis=1, keepdims=True) + EPS)


def per_device(
    queries, database, neighbour_ids, tile_weights, tile_columns, tile_owner, tile_block
):
    rows_dev = database.shape[0]
    feature_width = database.shape[1]
    unit_query = unit_rows(queries.astype(jnp.float32)).astype(jnp.bfloat16)
    first_row = lax.axis_index(("region", "shard")) * rows_dev
    similar = lax.dot_general(
        unit_query, database, (((1,), (1,)), ((), ())), preferred_element_type=jnp.float32
    )
    positive = jnp.maximum(similar, 0.0)
    weights = (positive * positive * positive / math.sqrt(feature_width)).astype(jnp.bfloat16)
    local_ids = neighbour_ids - first_row
    row_ids = lax.broadcasted_iota(jnp.int32, (1, 1, rows_dev), 2)
    counts = jnp.sum((local_ids[:, :, None] == row_ids).astype(jnp.float32), axis=1)
    chosen = (counts * weights.astype(jnp.float32)).astype(jnp.bfloat16)
    local_term = jnp.dot(chosen, database, preferred_element_type=jnp.float32)
    expanded_sum = lax.psum(local_term, ("region", "shard")) + unit_query.astype(jnp.float32)
    expanded = unit_rows(expanded_sum).astype(jnp.bfloat16)
    products = lax.dot_general(
        expanded, database, (((1,), (1,)), ((), ())), preferred_element_type=jnp.float32
    )
    scores = jnp.maximum(products, 0.0).astype(jnp.bfloat16)
    blocks_dev = tile_columns.shape[0]
    tile_count = tile_columns.shape[1]
    edge_count = tile_columns.shape[2]
    block_rows = tile_columns.shape[3]
    query_count = scores.shape[0]
    score_blocks = scores.reshape(query_count, blocks_dev, block_rows)
    owners = tile_owner.reshape(-1)
    block_ids = tile_block.reshape(-1)
    sources = owners * blocks_dev + block_ids

    def fetch_blocks(current):
        region_blocks = lax.all_gather(current, "shard", axis=1, tiled=True)
        return region_blocks.reshape(query_count, -1)

    column_base = (sources * block_rows).reshape(blocks_dev, tile_count, 1, 1)
    flat_columns = column_base + tile_columns

    def spread(current):
        flat = fetch_blocks(current)
        total = jnp.zeros((query_count, blocks_dev, block_rows), jnp.float32)
        for edge in range(edge_count):
            reached = jnp.take(flat, flat_columns[:, :, edge, :], axis=1)
            scaled = (
                reached.astype(jnp.float32) * tile_weights[:, :, edge, :].astype(jnp.float32)[None]
            )
            total = total + jnp.sum(scaled, axis=2)
        return total

    source = score_blocks.astype(jnp.float32)
    current = score_blocks
    current = (source + BETA * spread(current)).astype(jnp.bfloat16)
    diffused = source + BETA * spread(current)
    return diffused.reshape(query_count, blocks_dev * block_rows)


def solution(mesh):
    placed = (
        P(),
        P(("region", "shard"), None),
        P(),
        P(("region", "shard"), None, None, None),
        P(("region", "shard"), None, None, None),
        P(("region", "shard"), None),
        P(("region", "shard"), None),
    )
    return jax.shard_map(
        per_device,
        mesh=mesh,
        in_specs=placed,
        out_specs=P(None, ("region", "shard")),
        check_vma=False,
    )
```

profile of v0, /device:TPU:0, one launch (start us, length us, event | category | flops | bytes accessed | tf_op | source)
XLA Modules:
  0.0 358.0 jit_solution(2654204438736871811)
XLA Ops:
  6.6 0.8 broadcast_subtract_fusion
  7.4 0.2 convert_reduce_fusion
  7.5 1.0 fusion.1
  8.6 2.3 fusion.8
  11.0 0.1 broadcast_add_fusion
  11.1 0.1 fusion.21
  11.1 0.1 compare_and_fusion
  11.3 0.1 fusion.22
  11.5 0.6 pad_clamp_fusion.2
  12.1 0.6 copy.164
  12.7 0.6 pad_clamp_fusion.1
  13.3 0.6 copy.172
  13.9 0.6 copy.179
  14.5 0.6 fusion.14
  15.2 0.6 fusion.12
  15.8 0.6 pad_clamp_fusion
  16.4 123.9 %all-reduce.2.cloned.1.call-done = f32[48,1024]{1,0:T(8,128)} async-done(((f32[48,1024]{1,0:T(8,128)}), f32[48,1024]{1,0:T(8,128)}) %all-reduce.2.cloned.1.call-update) | async-done | bytes 196624 | tf_op jit(solution)/shard_map/psum | solution.py:32
  140.3 1.1 multiply_reduce_fusion.8
  141.4 1.4 fusion
  142.8 25.9 %all_gather.6 = bf16[48,32,256]{2,0,1:T(8,128)(2,1)} all-gather(bf16[48,2,256]{2,0,1:T(8,128)(2,1)S(1)} %bitcast.89), channel_id=1, replica_groups=mesh['region'=2,'shard'=16] {'shard'}, dimensions={1}, use_global_device_ids=true | all-gather | bytes 835584 | tf_op jit(solution)/shard_map/all_gather | solution.py:49
  168.7 2.0 copy.158
  170.7 14.2 %gather_fusion = bf16[6656,48]{1,0:T(8,128)(2,1)} fusion(bf16[48,8192]{0,1:T(8,128)(2,1)S(1)} %bitcast.70, s32[7168]{0:T(1024)S(1)} %pad_clamp_fusion.3), kind=kCustom, calls=%fused_computation.clone | custom fusion | bytes 1304576 | tf_op jit(solution)/shard_map/jit(_take)/gather | solution.py:59
  184.9 5.3 %multiply_reduce_fusion.7 = f32[48,2,256]{0,2,1:T(8,128)S(1)} fusion(bf16[2,13,256,48]{3,2,1,0:T(8,128)(2,1)} %bitcast.84, f32[2,13,256]{2,1,0:T(8,128)S(1)} %get-tuple-element.29, pred[2,13,256]{2,1,0:T(8,128)(4,1)S(1)} %copy.154), kind=kLoop, calls=%fused_computation.15 | loop fusion | flops 1253376 | bytes 770560 | tf_op jit(solution)/shard_map/reduce_sum | solution.py:63
  190.2 0.1 copy.169
  190.3 15.4 %gather_fusion.1 = bf16[6656,48]{1,0:T(8,128)(2,1)} fusion(bf16[48,8192]{0,1:T(8,128)(2,1)S(1)} %bitcast.71, s32[7168]{0:T(1024)} %pad_clamp_fusion.2), kind=kCustom, calls=%fused_computation.1.clone | custom fusion | bytes 1304576 | tf_op jit(solution)/shard_map/jit(_take)/gather | solution.py:59
  205.7 5.4 %multiply_reduce_fusion.6 = f32[48,2,256]{0,2,1:T(8,128)S(1)} fusion(bf16[2,13,256,48]{3,2,1,0:T(8,128)(2,1)} %bitcast.83, f32[2,13,256]{2,1,0:T(8,128)} %get-tuple-element.28, pred[2,13,256]{2,1,0:T(8,128)(4,1)} %copy.164), kind=kLoop, calls=%fused_computation.14 | loop fusion | flops 1253376 | bytes 770560 | tf_op jit(solution)/shard_map/reduce_sum | solution.py:63
  211.1 0.7 copy.170
  211.8 15.4 %gather_fusion.2 = bf16[6656,48]{1,0:T(8,128)(2,1)} fusion(bf16[48,8192]{0,1:T(8,128)(2,1)S(1)} %bitcast.72, s32[7168]{0:T(1024)} %pad_clamp_fusion.1), kind=kCustom, calls=%fused_computation.2.clone | custom fusion | bytes 1304576 | tf_op jit(solution)/shard_map/jit(_take)/gather | solution.py:59
  227.2 5.4 %multiply_reduce_fusion.5 = f32[48,2,256]{0,2,1:T(8,128)S(1)} fusion(bf16[2,13,256,48]{3,2,1,0:T(8,128)(2,1)} %bitcast.85, f32[2,13,256]{2,1,0:T(8,128)} %get-tuple-element.27, pred[2,13,256]{2,1,0:T(8,128)(4,1)} %copy.172), kind=kLoop, calls=%fused_computation.13 | loop fusion | flops 1253376 | bytes 770560 | tf_op jit(solution)/shard_map/reduce_sum | solution.py:63
  232.6 0.8 copy.177
  233.4 15.5 %gather_fusion.3 = bf16[6656,48]{1,0:T(8,128)(2,1)} fusion(bf16[48,8192]{0,1:T(8,128)(2,1)S(1)} %bitcast.73, s32[7168]{0:T(1024)} %pad_clamp_fusion), kind=kCustom, calls=%fused_computation.3.clone | custom fusion | bytes 1304576 | tf_op jit(solution)/shard_map/jit(_take)/gather | solution.py:59
  248.9 5.4 %multiply_reduce_fusion.4 = f32[48,2,256]{0,2,1:T(8,128)S(1)} fusion(bf16[2,13,256,48]{3,2,1,0:T(8,128)(2,1)} %bitcast.82, f32[2,13,256]{2,1,0:T(8,128)S(1)} %copy-done.11, pred[2,13,256]{2,1,0:T(8,128)(4,1)S(1)} %copy-done.22), kind=kLoop, calls=%fused_computation.12 | loop fusion | flops 1253376 | bytes 770560 | tf_op jit(solution)/shard_map/reduce_sum | solution.py:63
  254.3 0.1 copy.184
  254.5 21.0 %all_gather.7 = bf16[48,32,256]{2,0,1:T(8,128)(2,1)} all-gather(bf16[48,2,256]{2,0,1:T(8,128)(2,1)S(1)} %add_convert_fusion), channel_id=1, replica_groups=mesh['region'=2,'shard'=16] {'shard'}, dimensions={1}, use_global_device_ids=true | all-gather | bytes 835584 | tf_op jit(solution)/shard_map/all_gather | solution.py:49
  275.5 2.0 copy.185
  277.5 14.2 %gather_fusion.4 = bf16[6656,48]{1,0:T(8,128)(2,1)} fusion(bf16[48,8192]{0,1:T(8,128)(2,1)S(1)} %bitcast.74, s32[7168]{0:T(1024)S(1)} %copy-done.7), kind=kCustom, calls=%fused_computation.4.clone | custom fusion | bytes 1304576 | tf_op jit(solution)/shard_map/jit(_take)/gather | solution.py:59
  291.6 14.1 %gather_fusion.5 = bf16[6656,48]{1,0:T(8,128)(2,1)} fusion(bf16[48,8192]{0,1:T(8,128)(2,1)S(1)} %bitcast.75, s32[7168]{0:T(1024)S(1)} %copy-done.8), kind=kCustom, calls=%fused_computation.5.clone | custom fusion | bytes 1304576 | tf_op jit(solution)/shard_map/jit(_take)/gather | solution.py:59
  305.8 14.1 %gather_fusion.6 = bf16[6656,48]{1,0:T(8,128)(2,1)} fusion(bf16[48,8192]{0,1:T(8,128)(2,1)S(1)} %bitcast.76, s32[7168]{0:T(1024)S(1)} %copy-done.9), kind=kCustom, calls=%fused_computation.6.clone | custom fusion | bytes 1304576 | tf_op jit(solution)/shard_map/jit(_take)/gather | solution.py:59
  319.9 14.2 %gather_fusion.7 = bf16[6656,48]{1,0:T(8,128)(2,1)} fusion(bf16[48,8192]{0,1:T(8,128)(2,1)S(1)} %bitcast.77, s32[7168]{0:T(1024)S(1)} %copy-done.10), kind=kCustom, calls=%fused_computation.7.clone | custom fusion | bytes 1304576 | tf_op jit(solution)/shard_map/jit(_take)/gather | solution.py:59
  334.1 5.5 %multiply_reduce_fusion.3 = f32[48,2,256]{0,2,1:T(8,128)S(1)} fusion(bf16[2,13,256,48]{3,2,1,0:T(8,128)(2,1)} %bitcast.81, f32[2,13,256]{2,1,0:T(8,128)S(1)} %copy-done.15, pred[2,13,256]{2,1,0:T(8,128)(4,1)S(1)} %copy-done.19), kind=kLoop, calls=%fused_computation.11 | loop fusion | flops 1253376 | bytes 770560 | tf_op jit(solution)/shard_map/reduce_sum | solution.py:63
  339.6 0.1 copy.189
  339.7 2.4 multiply_reduce_fusion.2
  342.2 0.1 copy.190
  342.3 5.4 %multiply_reduce_fusion.1 = f32[48,2,256]{0,2,1:T(8,128)S(1)} fusion(bf16[2,13,256,48]{3,2,1,0:T(8,128)(2,1)} %bitcast.79, f32[2,13,256]{2,1,0:T(8,128)S(1)} %copy-done.12, pred[2,13,256]{2,1,0:T(8,128)(4,1)S(1)} %copy-done.21), kind=kLoop, calls=%fused_computation.9 | loop fusion | flops 1253376 | bytes 770560 | tf_op jit(solution)/shard_map/reduce_sum | solution.py:63
  347.7 0.1 copy.193
  347.9 2.4 multiply_reduce_fusion
  350.3 0.1 copy.196
  350.5 0.7 convert_add_fusion.1
  (72 shorter events, 0.4 us)
Async XLA Ops:
  6.5 2.0 copy-start
  6.5 4.4 %copy-start.25 = (s32[2,13]{1,0:T(2,128)S(1)}, s32[2,13]{1,0:T(2,128)}, u32[]{:S(2)}) copy-start(s32[2,13]{1,0:T(2,128)} %param.14) | copy-start | bytes 316
  6.5 4.4 %copy-start.24 = (s32[2,13]{1,0:T(2,128)S(1)}, s32[2,13]{1,0:T(2,128)}, u32[]{:S(2)}) copy-start(s32[2,13]{1,0:T(2,128)} %param.15) | copy-start | bytes 316
  6.5 4.4 %copy-start.17 = (s32[2,13,4,256]{3,2,1,0:T(4,128)S(1)}, s32[2,13,4,256]{3,2,1,0:T(4,128)}, u32[]{:S(2)}) copy-start(s32[2,13,4,256]{3,2,1,0:T(4,128)} %param.13) | copy-start | bytes 319492
  6.5 133.7 %all-reduce.2.cloned.1.call-start = ((), (), s32[]{:S(2)}) async-start(), calls=%async_computation | async-start | bytes 393216 | tf_op jit(solution)/shard_map/psum | solution.py:32
  8.6 2.7 copy-start.16
  10.9 129.4 %copy-start.3 = (bf16[48,1024]{1,0:T(8,128)(2,1)S(1)}, bf16[48,1024]{1,0:T(8,128)(2,1)}, u32[]{:S(2)}) copy-start(bf16[48,1024]{1,0:T(8,128)(2,1)} %param.9) | copy-start | bytes 294916
  11.3 159.5 %copy-start.6 = (s32[7168]{0:T(1024)}, s32[7168]{0:T(1024)S(1)}, u32[]{:S(2)}) copy-start(s32[7168]{0:T(1024)S(1)} %pad_clamp_fusion.3) | copy-start | bytes 86020
  11.3 173.6 %copy-start.18 = (pred[2,13,256]{2,1,0:T(8,128)(4,1)}, pred[2,13,256]{2,1,0:T(8,128)(4,1)S(1)}, u32[]{:S(2)}) copy-start(pred[2,13,256]{2,1,0:T(8,128)(4,1)S(1)} %copy.154) | copy-start | bytes 19972
  15.2 169.7 %copy-start.14 = (f32[2,13,256]{2,1,0:T(8,128)}, f32[2,13,256]{2,1,0:T(8,128)S(1)}, u32[]{:S(2)}) copy-start(f32[2,13,256]{2,1,0:T(8,128)S(1)} %get-tuple-element.29) | copy-start | bytes 79876
  233.4 15.5 %copy-start.11 = (f32[2,13,256]{2,1,0:T(8,128)S(1)}, f32[2,13,256]{2,1,0:T(8,128)}, u32[]{:S(2)}) copy-start(f32[2,13,256]{2,1,0:T(8,128)} %get-tuple-element.26) | copy-start | bytes 79876
  233.4 15.5 %copy-start.22 = (pred[2,13,256]{2,1,0:T(8,128)(4,1)S(1)}, pred[2,13,256]{2,1,0:T(8,128)(4,1)}, u32[]{:S(2)}) copy-start(pred[2,13,256]{2,1,0:T(8,128)(4,1)} %copy.179) | copy-start | bytes 19972
  248.9 5.5 %copy-start.4 = (f32[48,2,256]{2,0,1:T(8,128)S(1)}, f32[48,2,256]{2,0,1:T(8,128)}, u32[]{:S(2)}) copy-start(f32[48,2,256]{2,0,1:T(8,128)} %copy.170) | copy-start | bytes 294916
  248.9 5.5 %copy-start.5 = (f32[48,2,256]{2,0,1:T(8,128)S(1)}, f32[48,2,256]{2,0,1:T(8,128)}, u32[]{:S(2)}) copy-start(f32[48,2,256]{2,0,1:T(8,128)} %copy.177) | copy-start | bytes 294916
  254.4 23.0 %copy-start.7 = (s32[7168]{0:T(1024)S(1)}, s32[7168]{0:T(1024)}, u32[]{:S(2)}) copy-start(s32[7168]{0:T(1024)} %copy-done.6) | copy-start | bytes 86020
  277.5 14.2 %copy-start.8 = (s32[7168]{0:T(1024)S(1)}, s32[7168]{0:T(1024)}, u32[]{:S(2)}) copy-start(s32[7168]{0:T(1024)} %pad_clamp_fusion.2) | copy-start | bytes 86020
  291.6 14.1 %copy-start.9 = (s32[7168]{0:T(1024)S(1)}, s32[7168]{0:T(1024)}, u32[]{:S(2)}) copy-start(s32[7168]{0:T(1024)} %pad_clamp_fusion.1) | copy-start | bytes 86020
  305.8 14.2 %copy-start.10 = (s32[7168]{0:T(1024)S(1)}, s32[7168]{0:T(1024)}, u32[]{:S(2)}) copy-start(s32[7168]{0:T(1024)} %pad_clamp_fusion) | copy-start | bytes 86020
  319.9 14.2 %copy-start.15 = (f32[2,13,256]{2,1,0:T(8,128)S(1)}, f32[2,13,256]{2,1,0:T(8,128)}, u32[]{:S(2)}) copy-start(f32[2,13,256]{2,1,0:T(8,128)} %copy-done.14) | copy-start | bytes 79876
  319.9 14.2 %copy-start.19 = (pred[2,13,256]{2,1,0:T(8,128)(4,1)S(1)}, pred[2,13,256]{2,1,0:T(8,128)(4,1)}, u32[]{:S(2)}) copy-start(pred[2,13,256]{2,1,0:T(8,128)(4,1)} %copy-done.18) | copy-start | bytes 19972
  334.1 5.6 %copy-start.2 = (bf16[6656,48]{1,0:T(8,128)(2,1)S(1)}, bf16[6656,48]{1,0:T(8,128)(2,1)}, u32[]{:S(2)}) copy-start(bf16[6656,48]{1,0:T(8,128)(2,1)} %gather_fusion.5) | copy-start | bytes 1916932
  334.1 5.6 %copy-start.13 = (f32[2,13,256]{2,1,0:T(8,128)S(1)}, f32[2,13,256]{2,1,0:T(8,128)}, u32[]{:S(2)}) copy-start(f32[2,13,256]{2,1,0:T(8,128)} %get-tuple-element.28) | copy-start | bytes 79876
  334.1 5.6 %copy-start.20 = (pred[2,13,256]{2,1,0:T(8,128)(4,1)S(1)}, pred[2,13,256]{2,1,0:T(8,128)(4,1)}, u32[]{:S(2)}) copy-start(pred[2,13,256]{2,1,0:T(8,128)(4,1)} %copy.164) | copy-start | bytes 19972
  339.6 2.7 copy-start.12
  339.6 2.7 copy-start.21
  342.1 5.7 %copy-start.1 = (bf16[6656,48]{1,0:T(8,128)(2,1)S(1)}, bf16[6656,48]{1,0:T(8,128)(2,1)}, u32[]{:S(2)}) copy-start(bf16[6656,48]{1,0:T(8,128)(2,1)} %gather_fusion.7) | copy-start | bytes 1916932
  342.2 5.7 %copy-start.23 = (pred[2,13,256]{2,1,0:T(8,128)(4,1)S(1)}, pred[2,13,256]{2,1,0:T(8,128)(4,1)}, u32[]{:S(2)}) copy-start(pred[2,13,256]{2,1,0:T(8,128)(4,1)} %copy.179) | copy-start | bytes 19972
Sparse Core Ops, SparseCore 0:
  12.9 127.3 all-reduce.1
where the time goes:
time: 360 us; the launch traced here: 358 us
  local copies, waits for them, and re-layouts  125 us (35%)
  waiting for transfers between devices  124 us (34%)
  blocking collectives  46.9 us (13%)
  other arithmetic  44.3 us (12%)
  between operations  13.9 us (4%)
  matrix products  3.67 us (1%)
    psum x1, waiting for transfers between devices, per_device(): lax.psum(local_term, ('region', 'shard')) + unit_query.astype(jnp.float32)  124 us
    gather x8, local copies, waits for them, and re-layouts, spread(): reached = jnp.take(flat, flat_columns[:, :, edge, :], axis=1)  117 us
    all_gather x2, blocking collectives, fetch_blocks(): region_blocks = lax.all_gather(current, 'shard', axis=1, tiled=True)  46.9 us
    reduce_sum x8, other arithmetic, spread(): total = total + jnp.sum(scaled, axis=2)  37.2 us
  transfers between devices with their start and end apart: 1, of which 1 were waited for; matrix products, arithmetic and copies ran while one was open for 1% of the time, Pallas kernels for 0%

commit v1 on v0

--- a/solution.py
+++ b/solution.py
@@ -6,6 +6,29 @@
 
 EPS = 1e-06
 BETA = 0.8
+
+
+def balance_tails(incoming_x, where_dim):
+    big = list(incoming_x.shape[1:])
+    big[where_dim] *= incoming_x.shape[0]
+    extra = jnp.moveaxis(incoming_x, 0, where_dim).reshape(big)
+    return extra
+
+
+def switch_frames_now(obj, named_axis):
+    last = jax.lax.axis_size(named_axis)
+    u_next = jax.lax.axis_index(named_axis)
+    parts_out, z1 = (last, u_next)
+    newest, arr_next = (obj[None], 1)
+    while arr_next < parts_out:
+        pool = []
+        for at in range(parts_out):
+            pool.append((at, at ^ arr_next))
+        now = jax.lax.ppermute(newest, named_axis, pool)
+        res = z1 & arr_next == 0
+        newest = jnp.concatenate([jnp.where(res, newest, now), jnp.where(res, now, newest)])
+        arr_next *= 2
+    return newest
 
 
 def unit_rows(matrix):
@@ -46,7 +69,7 @@
     sources = owners * blocks_dev + block_ids
 
     def fetch_blocks(current):
-        region_blocks = lax.all_gather(current, "shard", axis=1, tiled=True)
+        region_blocks = balance_tails(switch_frames_now(current, "shard"), 1)
         return region_blocks.reshape(query_count, -1)
 
     column_base = (sources * block_rows).reshape(blocks_dev, tile_count, 1, 1)

time: 360 us -> 361 us (level)
  waiting for transfers between devices: 124 us -> 183 us
  blocking collectives: 46.9 us -> 0 us
  other arithmetic: 44.3 us -> 31.9 us
  starting transfers between devices: 0.03 us -> 9.77 us
  local copies, waits for them, and re-layouts: 125 us -> 118 us
    ppermute x0 -> x8, waiting for transfers between devices: none -> 54.2 us  [switch_frames_now(): now = jax.lax.ppermute(newest, named_axis, pool)]
    all_gather x2 -> x0, blocking collectives: 46.9 us -> none  [fetch_blocks(): region_blocks = lax.all_gather(current, 'shard', axis=1, tiled=True)]
    reduce_sum x8, other arithmetic: 37.2 us -> 25.4 us  [spread(): total = total + jnp.sum(scaled, axis=2)]
    ppermute x0 -> x8, starting transfers between devices: none -> 9.73 us  [switch_frames_now(): now = jax.lax.ppermute(newest, named_axis, pool)]
    psum x1, waiting for transfers between devices: 124 us -> 129 us  [per_device(): lax.psum(local_term, ('region', 'shard')) + unit_query.astype(jnp.float32)]
    all_gather x2 -> x0, local copies, waits for them, and re-layouts: 3.95 us -> none  [fetch_blocks(): region_blocks = lax.all_gather(current, 'shard', axis=1, tiled=True)]
    transpose x0 -> x2, local copies, waits for them, and re-layouts: none -> 3.95 us  [balance_tails(): extra = jnp.moveaxis(incoming_x, 0, where_dim).reshape(big)]
    gather x8, local copies, waits for them, and re-layouts: 117 us -> 113 us  [spread(): reached = jnp.take(flat, flat_columns[:, :, edge, :], axis=1)]
  transfers between devices with their start and end apart: 1 -> 9, of which waited for: 1 -> 9; matrix products, arithmetic and copies ran while one was open for 1% -> 0% of each run, Pallas kernels for 0% -> 0%
where the time goes in v1:
time: 361 us
  waiting for transfers between devices  183 us (51%)
  local copies, waits for them, and re-layouts  118 us (33%)
  other arithmetic  31.9 us (9%)
  between operations  14 us (4%)
  starting transfers between devices  9.77 us (3%)
  matrix products  3.72 us (1%)
    psum x1, waiting for transfers between devices, per_device(): lax.psum(local_term, ('region', 'shard')) + unit_query.astype(jnp.float32)  129 us
    gather x8, local copies, waits for them, and re-layouts, spread(): reached = jnp.take(flat, flat_columns[:, :, edge, :], axis=1)  113 us
    ppermute x8, waiting for transfers between devices, switch_frames_now(): now = jax.lax.ppermute(newest, named_axis, pool)  54.2 us
    reduce_sum x8, other arithmetic, spread(): total = total + jnp.sum(scaled, axis=2)  25.4 us
    ppermute x8, starting transfers between devices, switch_frames_now(): now = jax.lax.ppermute(newest, named_axis, pool)  9.73 us
  transfers between devices with their start and end apart: 9, of which 9 were waited for; matrix products, arithmetic and copies ran while one was open for 0% of the time, Pallas kernels for 0%

profile of v1, /device:TPU:0, one launch (start us, length us, event | category | flops | bytes accessed | tf_op | source)
XLA Modules:
  0.0 360.9 jit_solution(17580972214215145559)
XLA Ops:
  6.6 0.8 broadcast_subtract_fusion
  7.4 0.2 convert_reduce_fusion
  7.6 1.0 fusion.2
  8.6 2.3 fusion.9
  11.5 128.8 %all-reduce.2.cloned.1.call-done = f32[48,1024]{1,0:T(8,128)} async-done(((f32[48,1024]{1,0:T(8,128)}), f32[48,1024]{1,0:T(8,128)}) %all-reduce.2.cloned.1.call-update) | async-done | bytes 196624 | tf_op jit(solution)/shard_map/psum | solution.py:55
  140.3 1.1 multiply_reduce_fusion.8
  141.5 1.4 fusion
  142.9 0.1 copy.203
  143.2 0.3 copy-done.9
  143.5 0.9 collective-permute-done
  144.4 0.1 copy.162
  144.5 0.1 copy.163
  144.7 1.5 collective-permute-start.1
  146.2 3.4 collective-permute-done.1
  149.6 3.4 collective-permute-start.2
  153.0 4.4 %collective-permute-done.2 = bf16[4,48,2,256]{3,1,2,0:T(8,128)(2,1)S(1)} collective-permute-done((bf16[4,48,2,256]{3,1,2,0:T(8,128)(2,1)S(1)}, bf16[4,48,2,256]{3,1,2,0:T(8,128)(2,1)S(1)}, u32[]{:S(2)}, u32[]{:S(2)}) %collective-permute-start.2) | collective-permute-done | bytes 196640 | tf_op jit(solution)/shard_map/ppermute | solution.py:27
  157.5 1.8 collective-permute-start.3
  159.4 17.2 %collective-permute-done.3 = bf16[8,48,2,256]{3,1,2,0:T(8,128)(2,1)S(1)} collective-permute-done((bf16[8,48,2,256]{3,1,2,0:T(8,128)(2,1)S(1)}, bf16[8,48,2,256]{3,1,2,0:T(8,128)(2,1)S(1)}, u32[]{:S(2)}, u32[]{:S(2)}) %collective-permute-start.3) | collective-permute-done | bytes 393248 | tf_op jit(solution)/shard_map/ppermute | solution.py:27
  176.7 1.0 maximum_bitcast_fusion
  177.6 2.0 copy.164
  179.6 14.2 %gather_fusion.2 = bf16[6656,48]{1,0:T(8,128)(2,1)} fusion(bf16[48,8192]{0,1:T(8,128)(2,1)S(1)} %bitcast.75, s32[7168]{0:T(1024)S(1)} %pad_clamp_fusion.1), kind=kCustom, calls=%fused_computation.2.clone | custom fusion | bytes 1304576 | tf_op jit(solution)/shard_map/jit(_take)/gather | solution.py:82
  193.8 14.1 %gather_fusion.1 = bf16[6656,48]{1,0:T(8,128)(2,1)} fusion(bf16[48,8192]{0,1:T(8,128)(2,1)S(1)} %bitcast.76, s32[7168]{0:T(1024)S(1)} %pad_clamp_fusion.2), kind=kCustom, calls=%fused_computation.1.clone | custom fusion | bytes 1304576 | tf_op jit(solution)/shard_map/jit(_take)/gather | solution.py:82
  207.9 14.2 %gather_fusion = bf16[6656,48]{1,0:T(8,128)(2,1)} fusion(bf16[48,8192]{0,1:T(8,128)(2,1)S(1)} %bitcast.77, s32[7168]{0:T(1024)S(1)} %pad_clamp_fusion.3), kind=kCustom, calls=%fused_computation.clone | custom fusion | bytes 1304576 | tf_op jit(solution)/shard_map/jit(_take)/gather | solution.py:82
  222.1 14.1 %gather_fusion.3 = bf16[6656,48]{1,0:T(8,128)(2,1)} fusion(bf16[48,8192]{0,1:T(8,128)(2,1)S(1)} %bitcast.78, s32[7168]{0:T(1024)S(1)} %pad_clamp_fusion), kind=kCustom, calls=%fused_computation.3.clone | custom fusion | bytes 1304576 | tf_op jit(solution)/shard_map/jit(_take)/gather | solution.py:82
  236.2 5.5 %multiply_reduce_fusion.5 = f32[48,2,256]{0,2,1:T(8,128)S(1)} fusion(bf16[2,13,256,48]{3,2,1,0:T(8,128)(2,1)} %bitcast.86, f32[2,13,256]{2,1,0:T(8,128)S(1)} %get-tuple-element.43, pred[2,13,256]{2,1,0:T(8,128)(4,1)S(1)} %copy.176), kind=kLoop, calls=%fused_computation.13 | loop fusion | flops 1253376 | bytes 770560 | tf_op jit(solution)/shard_map/reduce_sum | solution.py:86
  241.7 2.4 multiply_reduce_fusion.6
  244.1 2.4 multiply_reduce_fusion.7
  246.6 2.4 multiply_reduce_fusion.4
  249.1 1.3 collective-permute-done.4
  250.5 0.1 copy.187
  250.6 0.1 copy.188
  250.7 1.5 collective-permute-start.5
  252.3 3.4 collective-permute-done.5
  255.8 6.1 %collective-permute-done.6 = bf16[4,48,2,256]{3,1,2,0:T(8,128)(2,1)S(1)} collective-permute-done((bf16[4,48,2,256]{3,1,2,0:T(8,128)(2,1)S(1)}, bf16[4,48,2,256]{3,1,2,0:T(8,128)(2,1)S(1)}, u32[]{:S(2)}, u32[]{:S(2)}) %collective-permute-start.6) | collective-permute-done | bytes 196640 | tf_op jit(solution)/shard_map/ppermute | solution.py:27
  261.9 1.2 collective-permute-start.7
  263.2 17.6 %collective-permute-done.7 = bf16[8,48,2,256]{3,1,2,0:T(8,128)(2,1)S(1)} collective-permute-done((bf16[8,48,2,256]{3,1,2,0:T(8,128)(2,1)S(1)}, bf16[8,48,2,256]{3,1,2,0:T(8,128)(2,1)S(1)}, u32[]{:S(2)}, u32[]{:S(2)}) %collective-permute-start.7) | collective-permute-done | bytes 393248 | tf_op jit(solution)/shard_map/ppermute | solution.py:27
  280.8 1.0 maximum_bitcast_fusion.1
  281.8 2.0 copy.189
  283.8 14.2 %gather_fusion.6 = bf16[6656,48]{1,0:T(8,128)(2,1)} fusion(bf16[48,8192]{0,1:T(8,128)(2,1)S(1)} %bitcast.71, s32[7168]{0:T(1024)S(1)} %pad_clamp_fusion.1), kind=kCustom, calls=%fused_computation.6.clone | custom fusion | bytes 1304576 | tf_op jit(solution)/shard_map/jit(_take)/gather | solution.py:82
  298.0 14.1 %gather_fusion.5 = bf16[6656,48]{1,0:T(8,128)(2,1)} fusion(bf16[48,8192]{0,1:T(8,128)(2,1)S(1)} %bitcast.72, s32[7168]{0:T(1024)S(1)} %pad_clamp_fusion.2), kind=kCustom, calls=%fused_computation.5.clone | custom fusion | bytes 1304576 | tf_op jit(solution)/shard_map/jit(_take)/gather | solution.py:82
  312.1 14.2 %gather_fusion.4 = bf16[6656,48]{1,0:T(8,128)(2,1)} fusion(bf16[48,8192]{0,1:T(8,128)(2,1)S(1)} %bitcast.73, s32[7168]{0:T(1024)S(1)} %pad_clamp_fusion.3), kind=kCustom, calls=%fused_computation.4.clone | custom fusion | bytes 1304576 | tf_op jit(solution)/shard_map/jit(_take)/gather | solution.py:82
  326.2 14.1 %gather_fusion.7 = bf16[6656,48]{1,0:T(8,128)(2,1)} fusion(bf16[48,8192]{0,1:T(8,128)(2,1)S(1)} %bitcast.74, s32[7168]{0:T(1024)S(1)} %pad_clamp_fusion), kind=kCustom, calls=%fused_computation.7.clone | custom fusion | bytes 1304576 | tf_op jit(solution)/shard_map/jit(_take)/gather | solution.py:82
  340.4 5.5 %multiply_reduce_fusion.1 = f32[48,2,256]{0,2,1:T(8,128)S(1)} fusion(bf16[2,13,256,48]{3,2,1,0:T(8,128)(2,1)} %bitcast.82, f32[2,13,256]{2,1,0:T(8,128)S(1)} %get-tuple-element.43, pred[2,13,256]{2,1,0:T(8,128)(4,1)S(1)} %copy.176), kind=kLoop, calls=%fused_computation.9 | loop fusion | flops 1253376 | bytes 770560 | tf_op jit(solution)/shard_map/reduce_sum | solution.py:86
  345.9 2.4 multiply_reduce_fusion.2
  348.3 2.4 multiply_reduce_fusion.3
  350.8 2.4 multiply_reduce_fusion
  353.2 0.1 copy.202
  353.4 0.7 convert_add_fusion.1
  (74 shorter events, 1.4 us)
Async XLA Ops:
  6.5 2.1 copy-start
  6.5 4.4 %copy-start.13 = (s32[2,13]{1,0:T(2,128)S(1)}, s32[2,13]{1,0:T(2,128)}, u32[]{:S(2)}) copy-start(s32[2,13]{1,0:T(2,128)} %param.14) | copy-start | bytes 316
  6.5 4.4 %copy-start.12 = (s32[2,13]{1,0:T(2,128)S(1)}, s32[2,13]{1,0:T(2,128)}, u32[]{:S(2)}) copy-start(s32[2,13]{1,0:T(2,128)} %param.15) | copy-start | bytes 316
  6.5 4.5 %copy-start.11 = (s32[2,13,4,256]{3,2,1,0:T(4,128)S(1)}, s32[2,13,4,256]{3,2,1,0:T(4,128)}, u32[]{:S(2)}) copy-start(s32[2,13,4,256]{3,2,1,0:T(4,128)} %param.13) | copy-start | bytes 319492
  6.5 4.7 %copy-start.8 = (bf16[2,13,4,256]{3,2,1,0:T(4,128)(2,1)S(1)}, bf16[2,13,4,256]{3,2,1,0:T(4,128)(2,1)}, u32[]{:S(2)}) copy-start(bf16[2,13,4,256]{3,2,1,0:T(4,128)(2,1)} %param.12) | copy-start | bytes 159748
  6.5 133.8 %all-reduce.2.cloned.1.call-start = ((), (), s32[]{:S(2)}) async-start(), calls=%async_computation | async-start | bytes 393216 | tf_op jit(solution)/shard_map/psum | solution.py:55
  8.6 131.7 %copy-start.7 = (bf16[48,1024]{1,0:T(8,128)(2,1)S(1)}, bf16[48,1024]{1,0:T(8,128)(2,1)}, u32[]{:S(2)}) copy-start(bf16[48,1024]{1,0:T(8,128)(2,1)} %param.9) | copy-start | bytes 294916
  142.9 0.6 copy-start.9
  143.0 1.4 collective-permute-start
  144.7 4.9 %collective-permute-start.1 = (bf16[2,48,2,256]{3,1,2,0:T(8,128)(2,1)S(1)}, bf16[2,48,2,256]{3,1,2,0:T(8,128)(2,1)S(1)}, u32[]{:S(2)}, u32[]{:S(2)}) collective-permute-start(bf16[2,48,2,256]{3,1,2,0:T(8,128)(2,1)S(1)} %pad_maximum_fusion.4), channel_id=1, source_target_pairs={{0,2},{1,3},{2,0},{3,1},{4,6},{5,7},{6,4},{7,5},{8,10},{9,11},{10,... | collective-permute-start | bytes 294920 | tf_op jit(solution)/shard_map/ppermute | solution.py:27
  149.6 7.8 %collective-permute-start.2 = (bf16[4,48,2,256]{3,1,2,0:T(8,128)(2,1)S(1)}, bf16[4,48,2,256]{3,1,2,0:T(8,128)(2,1)S(1)}, u32[]{:S(2)}, u32[]{:S(2)}) collective-permute-start(bf16[4,48,2,256]{3,1,2,0:T(8,128)(2,1)S(1)} %pad_maximum_fusion.2), channel_id=1, source_target_pairs={{0,4},{1,5},{2,6},{3,7},{4,0},{5,1},{6,2},{7,3},{8,12},{9,13},{10,... | collective-permute-start | bytes 589832 | tf_op jit(solution)/shard_map/ppermute | solution.py:27
  157.5 19.1 %collective-permute-start.3 = (bf16[8,48,2,256]{3,1,2,0:T(8,128)(2,1)S(1)}, bf16[8,48,2,256]{3,1,2,0:T(8,128)(2,1)S(1)}, u32[]{:S(2)}, u32[]{:S(2)}) collective-permute-start(bf16[8,48,2,256]{3,1,2,0:T(8,128)(2,1)S(1)} %pad_maximum_fusion), channel_id=1, source_target_pairs={{0,8},{1,9},{2,10},{3,11},{4,12},{5,13},{6,14},{7,15},{8,0},{9,1},... | collective-permute-start | bytes 1179656 | tf_op jit(solution)/shard_map/ppermute | solution.py:27
  236.2 5.5 %copy-start.6 = (bf16[6656,48]{1,0:T(8,128)(2,1)S(1)}, bf16[6656,48]{1,0:T(8,128)(2,1)}, u32[]{:S(2)}) copy-start(bf16[6656,48]{1,0:T(8,128)(2,1)} %gather_fusion.1) | copy-start | bytes 1916932
  236.2 7.9 %copy-start.5 = (bf16[6656,48]{1,0:T(8,128)(2,1)S(1)}, bf16[6656,48]{1,0:T(8,128)(2,1)}, u32[]{:S(2)}) copy-start(bf16[6656,48]{1,0:T(8,128)(2,1)} %gather_fusion) | copy-start | bytes 1916932
  241.7 4.9 %copy-start.4 = (bf16[6656,48]{1,0:T(8,128)(2,1)S(1)}, bf16[6656,48]{1,0:T(8,128)(2,1)}, u32[]{:S(2)}) copy-start(bf16[6656,48]{1,0:T(8,128)(2,1)} %gather_fusion.3) | copy-start | bytes 1916932
  249.1 1.4 collective-permute-start.4
  250.7 4.9 %collective-permute-start.5 = (bf16[2,48,2,256]{3,1,2,0:T(8,128)(2,1)S(1)}, bf16[2,48,2,256]{3,1,2,0:T(8,128)(2,1)S(1)}, u32[]{:S(2)}, u32[]{:S(2)}) collective-permute-start(bf16[2,48,2,256]{3,1,2,0:T(8,128)(2,1)S(1)} %pad_maximum_fusion.5), channel_id=1, source_target_pairs={{0,2},{1,3},{2,0},{3,1},{4,6},{5,7},{6,4},{7,5},{8,10},{9,11},{10,... | collective-permute-start | bytes 294920 | tf_op jit(solution)/shard_map/ppermute | solution.py:27
  255.7 6.2 %collective-permute-start.6 = (bf16[4,48,2,256]{3,1,2,0:T(8,128)(2,1)S(1)}, bf16[4,48,2,256]{3,1,2,0:T(8,128)(2,1)S(1)}, u32[]{:S(2)}, u32[]{:S(2)}) collective-permute-start(bf16[4,48,2,256]{3,1,2,0:T(8,128)(2,1)S(1)} %pad_maximum_fusion.3), channel_id=1, source_target_pairs={{0,4},{1,5},{2,6},{3,7},{4,0},{5,1},{6,2},{7,3},{8,12},{9,13},{10,... | collective-permute-start | bytes 589832 | tf_op jit(solution)/shard_map/ppermute | solution.py:27
  261.9 18.8 %collective-permute-start.7 = (bf16[8,48,2,256]{3,1,2,0:T(8,128)(2,1)S(1)}, bf16[8,48,2,256]{3,1,2,0:T(8,128)(2,1)S(1)}, u32[]{:S(2)}, u32[]{:S(2)}) collective-permute-start(bf16[8,48,2,256]{3,1,2,0:T(8,128)(2,1)S(1)} %pad_maximum_fusion.1), channel_id=1, source_target_pairs={{0,8},{1,9},{2,10},{3,11},{4,12},{5,13},{6,14},{7,15},{8,0},{9,1},... | collective-permute-start | bytes 1179656 | tf_op jit(solution)/shard_map/ppermute | solution.py:27
  340.4 5.5 %copy-start.3 = (bf16[6656,48]{1,0:T(8,128)(2,1)S(1)}, bf16[6656,48]{1,0:T(8,128)(2,1)}, u32[]{:S(2)}) copy-start(bf16[6656,48]{1,0:T(8,128)(2,1)} %gather_fusion.5) | copy-start | bytes 1916932
  340.4 7.9 %copy-start.2 = (bf16[6656,48]{1,0:T(8,128)(2,1)S(1)}, bf16[6656,48]{1,0:T(8,128)(2,1)}, u32[]{:S(2)}) copy-start(bf16[6656,48]{1,0:T(8,128)(2,1)} %gather_fusion.4) | copy-start | bytes 1916932
  345.9 4.9 %copy-start.1 = (bf16[6656,48]{1,0:T(8,128)(2,1)S(1)}, bf16[6656,48]{1,0:T(8,128)(2,1)}, u32[]{:S(2)}) copy-start(bf16[6656,48]{1,0:T(8,128)(2,1)} %gather_fusion.7) | copy-start | bytes 1916932
  350.8 2.6 copy-start.10
Sparse Core Ops, SparseCore 0:
  12.9 127.3 all-reduce.1
